TPU v7x, 32 devices: a whole 2x2x4 slice. The times are simulated.
32 devices in a mesh: dp: 8 (over y, x, core), mp: 4 (over z).
Axes of the slice: x: 2, y: 2, z: 4, core: 2. Of those that a mesh axis runs over, the one named last changes fastest.
Arguments:
- features: bfloat16 [4, 4096, 1152], P('mp', 'dp'), may hold values from -6 to 6
- context_gain: float32 [1152], replicated, may hold values from 0.1 to 1.9
- queries: bfloat16 [64, 1536], replicated, may hold values from -136 to 136
- w_key: bfloat16 [1152, 384], replicated, may hold values from -0.1875 to 0.1875
- w_value: bfloat16 [1152, 384], replicated, may hold values from -0.1875 to 0.1875
- w_out: bfloat16 [1536, 2048], replicated, may hold values from -0.15625 to 0.15625
- image_tiles: int32 [4, 2], P('mp'), may hold values from 1024 to 3072, as said below
- slot_start: int32 [4, 2], P('mp'), may hold values from 0 to 64
- text_rows: bfloat16 [4, 1024, 2048], P('mp', 'dp'), may hold values from -6 to 6
- row_grads: bfloat16 [4, 1024, 2048], P('mp', 'dp'), may hold values from -6 to 6
Outputs:
- merged_rows: bfloat16 [4, 1024, 2048], P('mp', 'dp')
- query_grad: float32 [64, 1536], replicated
Inputs may be any that keep to these rules, and one draw needn't show every extreme that they name: `image_tiles`: the 2 images of a group fill its 4096 rows in order; every image takes 2 * 512 to 3072 rows, and in every group one image takes exactly 1024 and one exactly 3072.
All inputs are finite; a program needn't handle non-finite values.
Results may differ from a plain program's by a relative error of at most 0.005.
The roundings to bfloat16 on the way count: a program that leaves them out, or rounds other values in their place, can miss the bound.
Values may be sent and summed in bfloat16 or wider, within the bound.
A program may use at most 128 MiB of HBM per device.

v0:
```python
import jax
import jax.numpy as jnp
from jax import lax
from jax.sharding import PartitionSpec as P

HEADS = 16
HEAD = 96
KVH = 4
LAT = 64
DM = 2048
TOK_DEV = 512
epsilon = 1e-06


def prefix_2(value, axis, join, neutral, backward):
    count, mine = (lax.axis_size(axis), lax.axis_index(axis))
    pieces = jax.tree.map(lambda part: lax.all_gather(part, axis), value)
    if backward:
        pieces = jax.tree.map(lambda part: part[::-1], pieces)
        mine = count - 1 - mine
    so_far = jax.tree.map(
        lambda part, zero: jnp.full_like(part, 0) + jnp.asarray(zero, part.dtype), value, neutral
    )

    def lap(position, so_far):
        longer = join(so_far, jax.tree.map(lambda part: part[position], pieces))
        return jax.tree.map(lambda new, old: jnp.where(position < mine, new, old), longer, so_far)

    return lax.fori_loop(0, count - 1, lap, so_far)


def normalize(features, context_gain):
    widened = features.astype(jnp.float32)
    mean_square = jnp.mean(widened * widened, axis=-1, keepdims=True)
    return (widened * lax.rsqrt(mean_square + epsilon) * context_gain).astype(jnp.bfloat16)


def merge_partials(earlier, later):
    early_id, early_peak, early_total, early_sum = earlier
    late_id, late_peak, late_total, late_sum = later
    joint_peak = jnp.maximum(early_peak, late_peak)
    early_scale = jnp.exp(early_peak - joint_peak)
    late_scale = jnp.exp(late_peak - joint_peak)
    joined = (
        late_id,
        joint_peak,
        early_total * early_scale + late_total * late_scale,
        early_sum * early_scale[..., None] + late_sum * late_scale[..., None],
    )
    same_image = early_id == late_id
    keep_early = late_id < 0
    return jax.tree.map(
        lambda early_value, joint_value, late_value: jnp.where(
            keep_early, early_value, jnp.where(same_image, joint_value, late_value)
        ),
        earlier,
        joined,
        later,
    )


def take_nearest(earlier, later):
    return jax.tree.map(
        lambda early_value, late_value: jnp.where(later[0] >= 0, late_value, early_value),
        earlier,
        later,
    )


def partial_sums(scores, value_heads, mask):
    masked = jnp.where(mask, scores, -jnp.inf)
    row_peak = jnp.max(masked, axis=-1)
    row_peak = jnp.where(jnp.any(mask), row_peak, 0.0)
    weights = jnp.where(mask, jnp.exp(scores - row_peak[..., None]), 0.0)
    weight_total = jnp.sum(weights, axis=-1)
    summed = jnp.einsum(
        "gclr,rge->gcle",
        weights.astype(jnp.bfloat16),
        value_heads,
        preferred_element_type=jnp.float32,
    )
    return (row_peak, weight_total, summed)


def to_heads(rows):
    return rows.reshape(LAT, KVH, HEADS // KVH, HEAD).transpose(1, 2, 0, 3)


def on_device(
    features,
    context_gain,
    queries,
    w_key,
    w_value,
    w_out,
    image_tiles,
    slot_start,
    text_rows,
    row_grads,
):
    group_heads = HEADS // KVH
    scale = HEAD ** (-0.5)
    normed = normalize(features[0], context_gain)
    key_heads = (
        jnp.dot(normed, w_key, preferred_element_type=jnp.float32)
        .astype(jnp.bfloat16)
        .reshape(TOK_DEV, KVH, HEAD)
    )
    value_heads = (
        jnp.dot(normed, w_value, preferred_element_type=jnp.float32)
        .astype(jnp.bfloat16)
        .reshape(TOK_DEV, KVH, HEAD)
    )
    query_heads = queries.reshape(LAT, KVH, group_heads, HEAD)
    scores = (
        jnp.einsum("lgce,rge->gclr", query_heads, key_heads, preferred_element_type=jnp.float32)
        * scale
    )
    device = lax.axis_index("dp")
    first_row = device * TOK_DEV
    image_ends = jnp.cumsum(image_tiles[0])
    positions = first_row + jnp.arange(TOK_DEV, dtype=jnp.int32)
    image_of = jnp.sum((positions[:, None] >= image_ends[None, :]).astype(jnp.int32), axis=1)
    first_image = image_of[0]
    last_image = image_of[-1]
    in_first = image_of == first_image
    in_last = (image_of == last_image) & (last_image != first_image)
    first_part = partial_sums(scores, value_heads, in_first)
    last_part = partial_sums(scores, value_heads, in_last)
    same_image = first_image == last_image
    running_part = jax.tree.map(
        lambda first_value, last_value: jnp.where(same_image, first_value, last_value),
        first_part,
        last_part,
    )
    element = (last_image.astype(jnp.float32),) + running_part
    stat_shape = (KVH, group_heads, LAT)
    identity = (
        jnp.full((), -1.0, jnp.float32),
        jnp.zeros(stat_shape, jnp.float32),
        jnp.zeros(stat_shape, jnp.float32),
        jnp.zeros(stat_shape + (HEAD,), jnp.float32),
    )
    prefix = prefix_2(element, "dp", merge_partials, identity, False)
    finished = merge_partials(prefix, (first_image.astype(jnp.float32),) + first_part)
    ends_here = image_ends[first_image] <= first_row + TOK_DEV
    attended = finished[3] / finished[2][..., None]
    attended_rows = attended.transpose(2, 0, 1, 3).reshape(LAT, HEADS * HEAD)
    projected = jnp.dot(
        attended_rows.astype(jnp.bfloat16), w_out, preferred_element_type=jnp.float32
    ).astype(jnp.bfloat16)
    slot_row = slot_start[0][first_image]
    placed = lax.dynamic_update_slice(text_rows[0], projected, (slot_row, jnp.int32(0)))
    merged = jnp.where(ends_here, placed, text_rows[0])[None]
    taken_rows = lax.dynamic_slice(row_grads[0], (slot_row, jnp.int32(0)), (LAT, DM))
    grad_rows = jnp.einsum(
        "ld,ed->le", taken_rows, w_out, preferred_element_type=jnp.float32
    ).astype(jnp.bfloat16)
    inner_dot = jnp.sum(to_heads(grad_rows.astype(jnp.float32)) * attended, axis=-1)
    valid_id = jnp.where(ends_here, first_image, -1).astype(jnp.float32)
    own_payload = (finished[1], finished[2], inner_dot, grad_rows)
    ident_whole = (
        jnp.full((), -1.0, jnp.float32),
        jnp.zeros(stat_shape, jnp.float32),
        jnp.zeros(stat_shape, jnp.float32),
        jnp.zeros(stat_shape, jnp.float32),
        jnp.zeros((LAT, HEADS * HEAD), jnp.float32),
    )
    suffix = prefix_2(
        (valid_id, finished[1], finished[2], inner_dot, grad_rows.astype(jnp.float32)),
        "dp",
        take_nearest,
        ident_whole,
        True,
    )
    far_payload = (suffix[1], suffix[2], suffix[3], suffix[4].astype(jnp.bfloat16))
    near_payload = jax.tree.map(
        lambda own_value, far_value: jnp.where(ends_here, own_value, far_value),
        own_payload,
        far_payload,
    )
    row_first = in_first[None, None, None, :]
    peak_rows = jnp.where(row_first, near_payload[0][..., None], far_payload[0][..., None])
    total_rows = jnp.where(row_first, near_payload[1][..., None], far_payload[1][..., None])
    inner_rows = jnp.where(row_first, near_payload[2][..., None], far_payload[2][..., None])
    probability = jnp.exp(scores - peak_rows) / total_rows
    dot_first = jnp.einsum(
        "gcle,rge->gclr", to_heads(near_payload[3]), value_heads, preferred_element_type=jnp.float32
    )
    dot_last = jnp.einsum(
        "gcle,rge->gclr", to_heads(far_payload[3]), value_heads, preferred_element_type=jnp.float32
    )
    chosen = jnp.where(row_first, dot_first, dot_last)
    score_grad = (probability * (chosen - inner_rows)).astype(jnp.bfloat16)
    grad_term = jnp.einsum(
        "gclr,rge->lgce", score_grad, key_heads, preferred_element_type=jnp.float32
    )
    grad_term = grad_term.reshape(LAT, HEADS * HEAD) * scale
    query_grad = lax.psum(grad_term, ("dp", "mp"))
    return (merged, query_grad)


def solution(mesh):
    placed = (
        P("mp", "dp", None),
        P(),
        P(),
        P(),
        P(),
        P(),
        P("mp", None),
        P("mp", None),
        P("mp", "dp", None),
        P("mp", "dp", None),
    )
    return jax.shard_map(
        on_device, mesh=mesh, in_specs=placed, out_specs=(P("mp", "dp", None), P()), check_vma=False
    )
```

profile of v0, /device:TPU:0, one launch (start us, length us, event | category | flops | bytes accessed | tf_op | source)
XLA Modules:
  0.0 310.1 jit_solution(13000130615180911)
XLA Ops:
  7.2 2.0 copy.83
  16.0 5.7 %convolution_convert_fusion = bf16[64,1536]{1,0:T(8,128)(2,1)} fusion(bf16[1536,2048]{1,0:T(8,128)(2,1)} %param.19, bf16[1,128,2048]{2,1,0:T(8,128)(2,1)} %param.23, s32[]{:T(128)S(6)} %select_n.443), kind=kOutput, calls=%fused_computation.23 | convolution fusion | flops 402751488 | bytes 6750212 | tf_op jit(solution)/shard_map/ld,ed->le/dot_general | solution.py:156
  25.7 2.1 fusion.67
  29.3 2.1 broadcast_select_fusion.7
  40.0 15.9 %all-reduce.2 = (f32[8]{0:T(128)}, f32[8]{0:T(128)S(1)}) all-reduce(f32[8]{0:T(128)S(1)} %dynamic-update-slice.2, f32[8]{0:T(128)S(1)} %dynamic-update-slice.3), channel_id=1, replica_groups=mesh['dp'=8,'mp'=4] {'dp'}, use_global_device_ids=true, to_apply=%add | all-reduce | flops 16 | bytes 128
  58.5 3.0 fusion.20
  61.5 8.3 %all-gather.1 = f32[32,4,64]{2,1,0:T(4,128)S(1)} all-gather(f32[4,4,64]{2,1,0:T(4,128)S(1)} %bitcast.201), channel_id=3, replica_groups=mesh['dp'=8,'mp'=4] {'dp'}, dimensions={0}, use_global_device_ids=true | all-gather | bytes 36864 | tf_op jit(solution)/shard_map/all_gather | solution.py:17
  69.8 9.4 %all-gather = f32[32,4,64]{2,1,0:T(4,128)S(1)} all-gather(f32[4,4,64]{2,1,0:T(4,128)S(1)} %copy-done.16), channel_id=2, replica_groups=mesh['dp'=8,'mp'=4] {'dp'}, dimensions={0}, use_global_device_ids=true | all-gather | bytes 36864 | tf_op jit(solution)/shard_map/all_gather | solution.py:17
  80.7 8.4 %all-gather.10.cloned.1.call-done = f32[32,4,64,96]{3,2,1,0:T(8,128)} async-done(((f32[4,4,64,96]{3,2,1,0:T(8,128)}), f32[32,4,64,96]{3,2,1,0:T(8,128)}) %all-gather.10.cloned.1.call-update) | async-done | bytes 3145744 | tf_op jit(solution)/shard_map/all_gather | solution.py:17
  89.1 33.9 %while.40 = (s32[]{:T(128)}, f32[]{:T(128)}, f32[4,4,64]{2,1,0:T(4,128)S(1)}, f32[4,4,64]{2,1,0:T(4,128)S(1)}, f32[4,4,64,96]{3,2,1,0:T(8,128)S(1)}, /*index=5*/...) while((s32[]{:T(128)}, f32[]{:T(128)}, ...), condition=%wide.region_10.11_spmd.clone, body=%wide.region_9.10_spmd.clone.sunk | while | flops 702472 | bytes 1220823 | solution.py:29
  91.7 1.6 select_select_fusion.14
  96.5 1.6 select_select_fusion.14
  101.4 1.6 select_select_fusion.14
  111.1 1.6 select_select_fusion.14
  120.8 1.6 select_select_fusion.14
  123.8 9.1 %all-gather.4 = f32[32,4,64]{2,1,0:T(4,128)S(1)} all-gather(f32[4,4,64]{2,1,0:T(4,128)S(1)} %bitcast.191), channel_id=6, replica_groups=mesh['dp'=8,'mp'=4] {'dp'}, dimensions={0}, use_global_device_ids=true | all-gather | bytes 36864 | tf_op jit(solution)/shard_map/all_gather | solution.py:17
  132.9 2.4 fusion.42
  135.3 8.4 %all-gather.5 = f32[32,4,64]{2,1,0:T(4,128)S(1)} all-gather(f32[4,4,64]{2,1,0:T(4,128)S(1)} %get-tuple-element.502), channel_id=7, replica_groups=mesh['dp'=8,'mp'=4] {'dp'}, dimensions={0}, use_global_device_ids=true | all-gather | bytes 36864 | tf_op jit(solution)/shard_map/all_gather | solution.py:17
  143.7 9.3 %all-gather.3 = f32[32,4,64]{2,1,0:T(4,128)S(1)} all-gather(f32[4,4,64]{2,1,0:T(4,128)S(1)} %bitcast.197), channel_id=5, replica_groups=mesh['dp'=8,'mp'=4] {'dp'}, dimensions={0}, use_global_device_ids=true | all-gather | bytes 36864 | tf_op jit(solution)/shard_map/all_gather | solution.py:17
  153.0 10.0 %while.41 = (s32[]{:T(128)}, f32[4,4,64]{2,1,0:T(4,128)S(1)}, f32[4,4,64]{2,1,0:T(4,128)S(1)}, f32[4,4,64]{2,1,0:T(4,128)S(1)}, bf16[64,1536]{1,0:T(8,128)(2,1)S...) while((s32[]{:T(128)}, f32[4,4,64]{2,1,0:T(4,128)S(1)}, ...), condition=%wide.region_13.14_spmd.clone, body=%wide.region_12.13_spmd.clone.sunk | while | flops 304133 | bytes 626881 | solution.py:29
  166.4 3.9 %fusion.25 = f32[64,4,4,96]{3,0,2,1:T(8,128)} fusion(bf16[512,4,96,1]{0,2,3,1:T(8,128)(2,1)} %bitcast.208, f32[4,4,64,512]{3,2,1,0:T(8,128)S(1)} %fusion.47, f32[4,512,64,4]{1,2,3,0:T(8,128)} %copy-done.1, bf16[512,4,96,1]{0,2,3,1:T(8,128)(2,1)S(1)} %bitcast.180, f32[4,4,64]{2,1,0:T(4,128)S(1)} %get-tuple-element.368, f32[4,4,64]{2,1,0:T(4,128)S(1)} %bitcast.203, ...), kind=kOutput, calls=%fused_computation.52 | convolution fusion | flops 206143488 | bytes 5595648 | tf_op jit(solution)/shard_map/gclr,rge->lgce/dot_general | solution.py:195
  173.4 4.0 %fusion.8 = bf16[1,64,2048]{2,1,0:T(8,128)(2,1)S(1)} fusion(bf16[64,1536]{1,0:T(8,128)(2,1)S(1)} %convert_element_type.70, bf16[1536,2048]{1,0:T(8,128)(2,1)} %param.19, bf16[1,128,2048]{2,1,0:T(8,128)(2,1)S(1)} %copy-done.6, s32[]{:T(128)S(6)} %select_n.443, pred[]{:T(512)S(6)} %le.3), kind=kOutput, calls=%fused_computation.26 | convolution fusion | flops 402915328 | bytes 7012357 | tf_op jit(solution)/shard_map/dot_general | solution.py:149
  178.8 123.0 %all-reduce.5.cloned.1.call-done = f32[64,1536]{1,0:T(8,128)} async-done(((f32[64,1536]{1,0:T(8,128)}), f32[64,1536]{1,0:T(8,128)}) %all-reduce.5.cloned.1.call-update) | async-done | bytes 393232 | tf_op jit(solution)/shard_map/psum | solution.py:199
  301.8 1.8 copy.85
  (144 shorter events, 41.4 us)
Async XLA Ops:
  7.2 20.6 %copy-start = (bf16[1152,384]{1,0:T(8,128)(2,1)S(1)}, bf16[1152,384]{1,0:T(8,128)(2,1)}, u32[]{:S(2)}) copy-start(bf16[1152,384]{1,0:T(8,128)(2,1)} %param.17) | copy-start | bytes 2654212
  7.2 72.0 %all-gather.12.cloned.1.call-start = ((), (), s32[]{:S(2)}) async-start(), calls=%async_computation.2 | async-start | bytes 1769472 | tf_op jit(solution)/shard_map/all_gather | solution.py:17
  16.0 8.4 %copy-start.12 = (bf16[64,1536]{1,0:T(8,128)(2,1)S(1)}, bf16[64,1536]{1,0:T(8,128)(2,1)}, u32[]{:S(2)}) copy-start(bf16[64,1536]{1,0:T(8,128)(2,1)} %param.16) | copy-start | bytes 589828
  16.0 9.4 %copy-start.8 = (bf16[1,512,1152]{2,1,0:T(8,128)(2,1)S(1)}, bf16[1,512,1152]{2,1,0:T(8,128)(2,1)}, u32[]{:S(2)}) copy-start(bf16[1,512,1152]{2,1,0:T(8,128)(2,1)} %param.14) | copy-start | bytes 3538948
  16.0 11.7 %copy-start.20 = (f32[1152]{0:T(1024)S(1)}, f32[1152]{0:T(1024)}, u32[]{:S(2)}) copy-start(f32[1152]{0:T(1024)} %param.15) | copy-start | bytes 13828
  21.7 67.4 %all-gather.10.cloned.1.call-start = ((), (), s32[]{:S(2)}) async-start(), calls=%async_computation.1 | async-start | bytes 4718592 | tf_op jit(solution)/shard_map/all_gather | solution.py:17
  25.7 3.0 copy-start.11
  27.7 30.7 %copy-start.17 = (pred[512]{0:T(512)(128)(4,1)}, pred[512]{0:T(512)(128)(4,1)S(1)}, u32[]{:S(2)}) copy-start(pred[512]{0:T(512)(128)(4,1)S(1)} %get-tuple-element.498) | copy-start | bytes 1540
  28.6 3.7 %copy-start.21 = (bf16[512,384]{0,1:T(8,128)(2,1)}, bf16[512,384]{0,1:T(8,128)(2,1)S(1)}, u32[]{:S(2)}) copy-start(bf16[512,384]{0,1:T(8,128)(2,1)S(1)} %convolution_convert_fusion.3) | copy-start | bytes 1179652
  28.6 2.8 copy-start.9
  28.6 2.8 copy-start.19
  29.3 3.6 %copy-start.1 = (f32[4,512,64,4]{1,2,3,0:T(8,128)}, f32[4,512,64,4]{1,2,3,0:T(8,128)S(1)}, u32[]{:S(2)}) copy-start(f32[4,512,64,4]{1,2,3,0:T(8,128)S(1)} %get-tuple-element.509) | copy-start | bytes 6291460
  31.4 27.1 %copy-start.13 = (f32[4,4,64]{2,1,0:T(4,128)}, f32[4,4,64]{2,1,0:T(4,128)S(1)}, u32[]{:S(2)}) copy-start(f32[4,4,64]{2,1,0:T(4,128)S(1)} %get-tuple-element.494) | copy-start | bytes 12292
  32.9 5.0 %copy-start.23 = (u32[32]{0:T(128)S(1)}, u32[32]{0:T(128)}, u32[]{:S(2)}) copy-start(u32[32]{0:T(128)} %constant.109) | copy-start | bytes 388
  32.9 23.7 %copy-start.2 = (bf16[64,1536]{1,0:T(8,128)(2,1)S(1)}, bf16[64,1536]{1,0:T(8,128)(2,1)}, u32[]{:S(2)}) copy-start(bf16[64,1536]{1,0:T(8,128)(2,1)} %convolution_convert_fusion) | copy-start | bytes 589828
  35.2 34.7 %copy-start.16 = (f32[4,4,64]{2,1,0:T(4,128)S(1)}, f32[4,4,64]{2,1,0:T(4,128)}, u32[]{:S(2)}) copy-start(f32[4,4,64]{2,1,0:T(4,128)} %get-tuple-element.492) | copy-start | bytes 12292
  35.2 266.6 %all-reduce.5.cloned.1.call-start = ((), (), s32[]{:S(2)}) async-start(), calls=%async_computation | async-start | bytes 786432 | tf_op jit(solution)/shard_map/psum | solution.py:199
  123.8 29.2 %copy-start.14 = (f32[2,8,64]{2,1,0:T(8,128)}, f32[2,8,64]{2,1,0:T(8,128)S(1)}, u32[]{:S(2)}) copy-start(f32[2,8,64]{2,1,0:T(8,128)S(1)} %get-tuple-element.536) | copy-start | bytes 12292
  123.8 29.2 %copy-start.22 = (f32[8]{0:T(128)S(1)}, f32[8]{0:T(128)}, u32[]{:S(2)}) copy-start(f32[8]{0:T(128)} %rev.15) | copy-start | bytes 100
  153.0 11.9 %copy-start.5 = (bf16[512,384]{0,1:T(8,128)(2,1)S(1)}, bf16[512,384]{0,1:T(8,128)(2,1)}, u32[]{:S(2)}) copy-start(bf16[512,384]{0,1:T(8,128)(2,1)} %copy-done.4) | copy-start | bytes 1179652
  163.0 3.3 %copy-start.15 = (f32[2,8,64]{2,1,0:T(8,128)S(1)}, f32[2,8,64]{2,1,0:T(8,128)}, u32[]{:S(2)}) copy-start(f32[2,8,64]{2,1,0:T(8,128)} %copy-done.14) | copy-start | bytes 12292
  163.0 3.3 %copy-start.18 = (pred[512]{0:T(512)(128)(4,1)S(1)}, pred[512]{0:T(512)(128)(4,1)}, u32[]{:S(2)}) copy-start(pred[512]{0:T(512)(128)(4,1)} %copy-done.17) | copy-start | bytes 1540
  170.2 3.2 %copy-start.6 = (bf16[1,128,2048]{2,1,0:T(8,128)(2,1)S(1)}, bf16[1,128,2048]{2,1,0:T(8,128)(2,1)}, u32[]{:S(2)}) copy-start(bf16[1,128,2048]{2,1,0:T(8,128)(2,1)} %copy.83) | copy-start | bytes 1572868
  178.8 124.8 %copy-start.7 = (bf16[1,128,2048]{2,1,0:T(8,128)(2,1)}, bf16[1,128,2048]{2,1,0:T(8,128)(2,1)S(1)}, u32[]{:S(2)}) copy-start(bf16[1,128,2048]{2,1,0:T(8,128)(2,1)S(1)} %select_n.447) | copy-start | bytes 1572868
  (3 other events, 4.3 us)
Sparse Core Ops, SparseCore 0:
  21.9 28.3 all-gather.11
  52.2 36.9 all-gather.9
  173.0 128.6 all-reduce.4
where the time goes:
time: 311 us; the launch traced here: 310 us
  waiting for transfers between devices  131 us (42%)
  blocking collectives  60.4 us (19%)
  local copies, waits for them, and re-layouts  32.7 us (11%)
  other arithmetic  24.4 us (8%)
  between operations  23.5 us (8%)
  matrix products  19.2 us (6%)
  loops' own time  18.3 us (6%)
    psum x1, waiting for transfers between devices, on_device(): query_grad = lax.psum(grad_term, ('dp', 'mp'))  123 us
    all_gather x5, blocking collectives, prefix_2(): pieces = jax.tree.map(lambda part: lax.all_gather(part, axis), value)  44.5 us
    another operation x2, loops' own time, prefix_2(): return lax.fori_loop(0, count - 1, lap, so_far)  18.3 us
    unnamed x1, blocking collectives  15.9 us
    select_n x35, other arithmetic, lap(): jnp.where(position < mine, new, old)  12.8 us
    dynamic_slice x14, local copies, waits for them, and re-layouts, lap(): longer = join(so_far, jax.tree.map(lambda part: part[position], pieces))  12.8 us
    all_gather x2, waiting for transfers between devices, prefix_2(): pieces = jax.tree.map(lambda part: lax.all_gather(part, axis), value)  8.4 us
    unnamed x55, local copies, waits for them, and re-layouts  6.75 us
  transfers between devices with their start and end apart: 3, of which 2 were waited for; matrix products, arithmetic and copies ran while one was open for 8% of the time, Pallas kernels for 0%

commit v1 on v0

--- a/solution.py
+++ b/solution.py
@@ -1,3 +1,4 @@
+import functools
 import jax
 import jax.numpy as jnp
 from jax import lax
@@ -10,6 +11,13 @@
 DM = 2048
 TOK_DEV = 512
 epsilon = 1e-06
+
+
+def try_all_spots(unit, mesh_dim):
+    return lax.all_gather(unit, axis_name=mesh_dim).sum(axis=0)
+
+
+refer_sample_now = functools.partial(try_all_spots, mesh_dim=("dp", "mp"))
 
 
 def prefix_2(value, axis, join, neutral, backward):
@@ -196,7 +204,7 @@
         "gclr,rge->lgce", score_grad, key_heads, preferred_element_type=jnp.float32
     )
     grad_term = grad_term.reshape(LAT, HEADS * HEAD) * scale
-    query_grad = lax.psum(grad_term, ("dp", "mp"))
+    query_grad = refer_sample_now(grad_term)
     return (merged, query_grad)
 
 

time: 311 us -> 282 us (0.907)
  waiting for transfers between devices: 131 us -> 98 us
  other arithmetic: 24.4 us -> 30.5 us
    psum x1 -> x0, waiting for transfers between devices: 123 us -> none  [on_device(): query_grad = lax.psum(grad_term, ('dp', 'mp'))]
    all_gather x0 -> x1, waiting for transfers between devices: none -> 89.5 us  [try_all_spots(): return lax.all_gather(unit, axis_name=mesh_dim).sum(axis=0)]
    reduce_sum x0 -> x1, other arithmetic: none -> 6.18 us  [try_all_spots(): return lax.all_gather(unit, axis_name=mesh_dim).sum(axis=0)]
    unnamed x55 -> x54, local copies, waits for them, and re-layouts: 6.75 us -> 5.15 us
  transfers between devices with their start and end apart: 3 -> 3, of which waited for: 2 -> 2; matrix products, arithmetic and copies ran while one was open for 8% -> 9% of each run, Pallas kernels for 0% -> 0%
where the time goes in v1:
time: 282 us; the launch traced here: 281 us
  waiting for transfers between devices  98 us (35%)
  blocking collectives  60.5 us (21%)
  local copies, waits for them, and re-layouts  31.2 us (11%)
  other arithmetic  30.5 us (11%)
  between operations  23.2 us (8%)
  matrix products  19.2 us (7%)
  loops' own time  17.9 us (6%)
    all_gather x1, waiting for transfers between devices, try_all_spots(): return lax.all_gather(unit, axis_name=mesh_dim).sum(axis=0)  89.5 us
    all_gather x5, blocking collectives, prefix_2(): pieces = jax.tree.map(lambda part: lax.all_gather(part, axis), value)  44.5 us
    another operation x2, loops' own time, prefix_2(): return lax.fori_loop(0, count - 1, lap, so_far)  17.9 us
    unnamed x1, blocking collectives  16 us
    dynamic_slice x14, local copies, waits for them, and re-layouts, lap(): longer = join(so_far, jax.tree.map(lambda part: part[position], pieces))  12.9 us
    select_n x35, other arithmetic, lap(): jnp.where(position < mine, new, old)  12.8 us
    all_gather x2, waiting for transfers between devices, prefix_2(): pieces = jax.tree.map(lambda part: lax.all_gather(part, axis), value)  8.39 us
    reduce_sum x1, other arithmetic, try_all_spots(): return lax.all_gather(unit, axis_name=mesh_dim).sum(axis=0)  6.18 us
  transfers between devices with their start and end apart: 3, of which 2 were waited for; matrix products, arithmetic and copies ran while one was open for 9% of the time, Pallas kernels for 0%

profile of v1, /device:TPU:0, one launch (start us, length us, event | category | flops | bytes accessed | tf_op | source)
XLA Modules:
  0.0 280.5 jit_solution(9328596093787081352)
XLA Ops:
  7.2 2.0 copy.83
  15.9 5.7 %convolution_convert_fusion = bf16[64,1536]{1,0:T(8,128)(2,1)} fusion(bf16[1536,2048]{1,0:T(8,128)(2,1)} %param.19, bf16[1,128,2048]{2,1,0:T(8,128)(2,1)} %param.23, s32[]{:T(128)S(6)} %select_n.443), kind=kOutput, calls=%fused_computation.23 | convolution fusion | flops 402751488 | bytes 6750212 | tf_op jit(solution)/shard_map/ld,ed->le/dot_general | solution.py:164
  25.5 2.1 fusion.67
  29.2 2.1 broadcast_select_fusion.7
  39.8 16.0 %all-reduce.2 = (f32[8]{0:T(128)}, f32[8]{0:T(128)S(1)}) all-reduce(f32[8]{0:T(128)S(1)} %dynamic-update-slice.2, f32[8]{0:T(128)S(1)} %dynamic-update-slice.3), channel_id=1, replica_groups=mesh['dp'=8,'mp'=4] {'dp'}, use_global_device_ids=true, to_apply=%add | all-reduce | flops 16 | bytes 128
  58.3 3.0 %fusion.20 = (f32[4,4,64]{2,1,0:T(4,128)S(1)}, f32[4,4,64]{2,1,0:T(4,128)S(1)}) fusion(f32[4,512,64,4]{1,2,3,0:T(8,128)} %copy-done.1, f32[4,4,64]{2,1,0:T(4,128)S(1)} %get-tuple-element.493, pred[512]{0:T(512)(128)(4,1)S(1)} %get-tuple-element.506, f32[4,4,64]{2,1,0:T(4,128)S(1)} %get-tuple-element.494, pred[512]{0:T(512)(128)(4,1)S(1)} %get-tuple-element.498), kind=kLoop, calls=%fused_computation.43 | loop fusion | flops 3143680 | bytes 2114560 | tf_op jit(solution)/shard_map/reduce_sum | solution.py:83
  61.3 8.3 %all-gather.1 = f32[32,4,64]{2,1,0:T(4,128)S(1)} all-gather(f32[4,4,64]{2,1,0:T(4,128)S(1)} %bitcast.201), channel_id=3, replica_groups=mesh['dp'=8,'mp'=4] {'dp'}, dimensions={0}, use_global_device_ids=true | all-gather | bytes 36864 | tf_op jit(solution)/shard_map/all_gather | solution.py:25
  69.6 9.4 %all-gather = f32[32,4,64]{2,1,0:T(4,128)S(1)} all-gather(f32[4,4,64]{2,1,0:T(4,128)S(1)} %copy-done.16), channel_id=2, replica_groups=mesh['dp'=8,'mp'=4] {'dp'}, dimensions={0}, use_global_device_ids=true | all-gather | bytes 36864 | tf_op jit(solution)/shard_map/all_gather | solution.py:25
  80.5 8.4 %all-gather.13.cloned.1.call-done = f32[32,4,64,96]{3,2,1,0:T(8,128)} async-done(((f32[4,4,64,96]{3,2,1,0:T(8,128)}), f32[32,4,64,96]{3,2,1,0:T(8,128)}) %all-gather.13.cloned.1.call-update) | async-done | bytes 3145744 | tf_op jit(solution)/shard_map/all_gather | solution.py:25
  88.9 34.2 %while.40 = (s32[]{:T(128)}, f32[]{:T(128)}, f32[4,4,64]{2,1,0:T(4,128)S(1)}, f32[4,4,64]{2,1,0:T(4,128)S(1)}, f32[4,4,64,96]{3,2,1,0:T(8,128)S(1)}, /*index=5*/...) while((s32[]{:T(128)}, f32[]{:T(128)}, ...), condition=%wide.region_10.11_spmd.clone, body=%wide.region_9.10_spmd.clone.sunk | while | flops 702472 | bytes 1220823 | solution.py:37
  91.5 1.6 select_select_fusion.14
  96.4 1.6 select_select_fusion.14
  101.3 1.6 select_select_fusion.14
  106.2 1.6 select_select_fusion.14
  120.8 1.6 select_select_fusion.14
  123.9 9.1 %all-gather.4 = f32[32,4,64]{2,1,0:T(4,128)S(1)} all-gather(f32[4,4,64]{2,1,0:T(4,128)S(1)} %bitcast.191), channel_id=6, replica_groups=mesh['dp'=8,'mp'=4] {'dp'}, dimensions={0}, use_global_device_ids=true | all-gather | bytes 36864 | tf_op jit(solution)/shard_map/all_gather | solution.py:25
  133.0 2.4 fusion.42
  135.4 8.4 %all-gather.5 = f32[32,4,64]{2,1,0:T(4,128)S(1)} all-gather(f32[4,4,64]{2,1,0:T(4,128)S(1)} %get-tuple-element.502), channel_id=7, replica_groups=mesh['dp'=8,'mp'=4] {'dp'}, dimensions={0}, use_global_device_ids=true | all-gather | bytes 36864 | tf_op jit(solution)/shard_map/all_gather | solution.py:25
  143.7 9.3 %all-gather.3 = f32[32,4,64]{2,1,0:T(4,128)S(1)} all-gather(f32[4,4,64]{2,1,0:T(4,128)S(1)} %bitcast.197), channel_id=5, replica_groups=mesh['dp'=8,'mp'=4] {'dp'}, dimensions={0}, use_global_device_ids=true | all-gather | bytes 36864 | tf_op jit(solution)/shard_map/all_gather | solution.py:25
  153.1 9.4 %while.41 = (s32[]{:T(128)}, f32[4,4,64]{2,1,0:T(4,128)S(1)}, f32[4,4,64]{2,1,0:T(4,128)S(1)}, f32[4,4,64]{2,1,0:T(4,128)S(1)}, bf16[64,1536]{1,0:T(8,128)(2,1)S...) while((s32[]{:T(128)}, f32[4,4,64]{2,1,0:T(4,128)S(1)}, ...), condition=%wide.region_13.14_spmd.clone, body=%wide.region_12.13_spmd.clone.sunk | while | flops 304133 | bytes 626881 | solution.py:37
  165.9 3.9 %fusion.25 = f32[64,4,4,96]{3,0,2,1:T(8,128)} fusion(bf16[512,4,96,1]{0,2,3,1:T(8,128)(2,1)} %bitcast.208, f32[4,4,64,512]{3,2,1,0:T(8,128)S(1)} %fusion.47, f32[4,512,64,4]{1,2,3,0:T(8,128)} %copy-done.1, bf16[512,4,96,1]{0,2,3,1:T(8,128)(2,1)S(1)} %bitcast.180, f32[4,4,64]{2,1,0:T(4,128)S(1)} %get-tuple-element.368, f32[4,4,64]{2,1,0:T(4,128)S(1)} %bitcast.203, ...), kind=kOutput, calls=%fused_computation.52 | convolution fusion | flops 206143488 | bytes 5595648 | tf_op jit(solution)/shard_map/gclr,rge->lgce/dot_general | solution.py:203
  172.9 4.0 %fusion.8 = bf16[1,64,2048]{2,1,0:T(8,128)(2,1)S(1)} fusion(bf16[64,1536]{1,0:T(8,128)(2,1)S(1)} %convert_element_type.70, bf16[1536,2048]{1,0:T(8,128)(2,1)} %param.19, bf16[1,128,2048]{2,1,0:T(8,128)(2,1)S(1)} %copy-done.6, s32[]{:T(128)S(6)} %select_n.443, pred[]{:T(512)S(6)} %le.3), kind=kOutput, calls=%fused_computation.26 | convolution fusion | flops 402915328 | bytes 7012357 | tf_op jit(solution)/shard_map/dot_general | solution.py:157
  178.3 89.5 %all-gather.11.cloned.1.call-done = f32[32,64,1536]{2,1,0:T(8,128)} async-done(((f32[1,64,1536]{2,1,0:T(8,128)}), f32[32,64,1536]{2,1,0:T(8,128)}) %all-gather.11.cloned.1.call-update) | async-done | bytes 12582928 | tf_op jit(solution)/shard_map/all_gather | solution.py:17
  267.8 6.2 %reduce_sum.59 = f32[64,1536]{1,0:T(8,128)} reduce(f32[32,64,1536]{2,1,0:T(8,128)} %all-gather.11.cloned.1.call-done, f32[]{:T(128)} %constant.92.clone.1), dimensions={0}, to_apply=%region_14.15 | reduce | flops 3047424 | bytes 12976132 | tf_op jit(solution)/shard_map/reduce_sum | solution.py:17
  (144 shorter events, 41.7 us)
Async XLA Ops:
  7.2 20.4 %copy-start = (bf16[1152,384]{1,0:T(8,128)(2,1)S(1)}, bf16[1152,384]{1,0:T(8,128)(2,1)}, u32[]{:S(2)}) copy-start(bf16[1152,384]{1,0:T(8,128)(2,1)} %param.17) | copy-start | bytes 2654212
  7.2 71.9 %all-gather.15.cloned.1.call-start = ((), (), s32[]{:S(2)}) async-start(), calls=%async_computation.2 | async-start | bytes 1769472 | tf_op jit(solution)/shard_map/all_gather | solution.py:25
  15.8 8.4 %copy-start.12 = (bf16[64,1536]{1,0:T(8,128)(2,1)S(1)}, bf16[64,1536]{1,0:T(8,128)(2,1)}, u32[]{:S(2)}) copy-start(bf16[64,1536]{1,0:T(8,128)(2,1)} %param.16) | copy-start | bytes 589828
  15.8 9.4 %copy-start.8 = (bf16[1,512,1152]{2,1,0:T(8,128)(2,1)S(1)}, bf16[1,512,1152]{2,1,0:T(8,128)(2,1)}, u32[]{:S(2)}) copy-start(bf16[1,512,1152]{2,1,0:T(8,128)(2,1)} %param.14) | copy-start | bytes 3538948
  15.8 11.8 %copy-start.20 = (f32[1152]{0:T(1024)S(1)}, f32[1152]{0:T(1024)}, u32[]{:S(2)}) copy-start(f32[1152]{0:T(1024)} %param.15) | copy-start | bytes 13828
  21.6 67.4 %all-gather.13.cloned.1.call-start = ((), (), s32[]{:S(2)}) async-start(), calls=%async_computation.1 | async-start | bytes 4718592 | tf_op jit(solution)/shard_map/all_gather | solution.py:25
  25.5 3.0 %copy-start.11 = (bf16[64,4,4,96]{3,2,1,0:T(4,128)(2,1)S(1)}, bf16[64,4,4,96]{3,2,1,0:T(4,128)(2,1)}, u32[]{:S(2)}) copy-start(bf16[64,4,4,96]{3,2,1,0:T(4,128)(2,1)} %reshape.130) | copy-start | bytes 589828
  27.6 30.7 %copy-start.17 = (pred[512]{0:T(512)(128)(4,1)}, pred[512]{0:T(512)(128)(4,1)S(1)}, u32[]{:S(2)}) copy-start(pred[512]{0:T(512)(128)(4,1)S(1)} %get-tuple-element.498) | copy-start | bytes 1540
  28.4 3.6 %copy-start.21 = (bf16[512,384]{0,1:T(8,128)(2,1)}, bf16[512,384]{0,1:T(8,128)(2,1)S(1)}, u32[]{:S(2)}) copy-start(bf16[512,384]{0,1:T(8,128)(2,1)S(1)} %convolution_convert_fusion.3) | copy-start | bytes 1179652
  28.5 2.8 copy-start.9
  28.5 2.8 copy-start.19
  29.1 3.5 %copy-start.1 = (f32[4,512,64,4]{1,2,3,0:T(8,128)}, f32[4,512,64,4]{1,2,3,0:T(8,128)S(1)}, u32[]{:S(2)}) copy-start(f32[4,512,64,4]{1,2,3,0:T(8,128)S(1)} %get-tuple-element.509) | copy-start | bytes 6291460
  31.2 27.1 %copy-start.13 = (f32[4,4,64]{2,1,0:T(4,128)}, f32[4,4,64]{2,1,0:T(4,128)S(1)}, u32[]{:S(2)}) copy-start(f32[4,4,64]{2,1,0:T(4,128)S(1)} %get-tuple-element.494) | copy-start | bytes 12292
  32.7 4.9 %copy-start.23 = (u32[32]{0:T(128)S(1)}, u32[32]{0:T(128)}, u32[]{:S(2)}) copy-start(u32[32]{0:T(128)} %constant.109) | copy-start | bytes 388
  32.7 23.8 %copy-start.2 = (bf16[64,1536]{1,0:T(8,128)(2,1)S(1)}, bf16[64,1536]{1,0:T(8,128)(2,1)}, u32[]{:S(2)}) copy-start(bf16[64,1536]{1,0:T(8,128)(2,1)} %convolution_convert_fusion) | copy-start | bytes 589828
  34.9 34.6 %copy-start.16 = (f32[4,4,64]{2,1,0:T(4,128)S(1)}, f32[4,4,64]{2,1,0:T(4,128)}, u32[]{:S(2)}) copy-start(f32[4,4,64]{2,1,0:T(4,128)} %get-tuple-element.492) | copy-start | bytes 12292
  35.0 232.8 %all-gather.11.cloned.1.call-start = ((), (), s32[]{:S(2)}) async-start(), calls=%async_computation | async-start | bytes 12976128 | tf_op jit(solution)/shard_map/all_gather | solution.py:17
  123.8 29.2 %copy-start.14 = (f32[2,8,64]{2,1,0:T(8,128)}, f32[2,8,64]{2,1,0:T(8,128)S(1)}, u32[]{:S(2)}) copy-start(f32[2,8,64]{2,1,0:T(8,128)S(1)} %get-tuple-element.536) | copy-start | bytes 12292
  123.8 29.2 %copy-start.22 = (f32[8]{0:T(128)S(1)}, f32[8]{0:T(128)}, u32[]{:S(2)}) copy-start(f32[8]{0:T(128)} %rev.15) | copy-start | bytes 100
  153.1 11.4 %copy-start.5 = (bf16[512,384]{0,1:T(8,128)(2,1)S(1)}, bf16[512,384]{0,1:T(8,128)(2,1)}, u32[]{:S(2)}) copy-start(bf16[512,384]{0,1:T(8,128)(2,1)} %copy-done.4) | copy-start | bytes 1179652
  162.5 3.3 %copy-start.15 = (f32[2,8,64]{2,1,0:T(8,128)S(1)}, f32[2,8,64]{2,1,0:T(8,128)}, u32[]{:S(2)}) copy-start(f32[2,8,64]{2,1,0:T(8,128)} %copy-done.14) | copy-start | bytes 12292
  162.5 3.3 %copy-start.18 = (pred[512]{0:T(512)(128)(4,1)S(1)}, pred[512]{0:T(512)(128)(4,1)}, u32[]{:S(2)}) copy-start(pred[512]{0:T(512)(128)(4,1)} %copy-done.17) | copy-start | bytes 1540
  169.7 3.2 %copy-start.6 = (bf16[1,128,2048]{2,1,0:T(8,128)(2,1)S(1)}, bf16[1,128,2048]{2,1,0:T(8,128)(2,1)}, u32[]{:S(2)}) copy-start(bf16[1,128,2048]{2,1,0:T(8,128)(2,1)} %copy.83) | copy-start | bytes 1572868
  178.3 95.7 %copy-start.7 = (bf16[1,128,2048]{2,1,0:T(8,128)(2,1)}, bf16[1,128,2048]{2,1,0:T(8,128)(2,1)S(1)}, u32[]{:S(2)}) copy-start(bf16[1,128,2048]{2,1,0:T(8,128)(2,1)S(1)} %select_n.447) | copy-start | bytes 1572868
  (3 other events, 4.3 us)
Sparse Core Ops, SparseCore 0:
  21.7 28.3 all-gather.14
  52.0 36.9 all-gather.12
  172.5 95.2 all-gather.10
